TPU v7x, 512 devices: a whole 4x8x8 slice. The times are simulated.
512 devices in a mesh: seq: 32 (over x, z), tp: 16 (over y, core).
Axes of the slice: x: 4, y: 8, z: 8, core: 2. Of those that a mesh axis runs over, the one named last changes fastest.
Arguments:
- residual: bfloat16 [6144, 8192], P('seq', 'tp'), may hold values from -6 to 6
- attention: bfloat16 [1536, 8192], P('seq'), may hold values from -6 to 6
- quantized_codes: int32 [8192, 8192], P('seq', 'tp'), may hold values from 0 to 15
- absmax: float32 [8192, 128], P('seq', 'tp'), may hold values from 0.005 to 0.05
- adapter_down: bfloat16 [8192, 64], P('seq'), may hold values from -0.0625 to 0.0625
- adapter_up: bfloat16 [64, 8192], P(None, 'tp'), may hold values from -0.75 to 0.75
- routed_slot_gate: float32 [1536], P('seq'), may hold values from 0.2 to 1
- selected: int32 [1536], P('seq'), may hold values from 0 to 191, as said below
- counts: int32 [32], P('seq'), may hold values from 1 to 48, 768 in all
- cotangent: bfloat16 [6144, 8192], P('seq', 'tp'), may hold values from -0.59765625 to 0.59765625
Outputs:
- outgoing_residual: bfloat16 [6144, 8192], P('seq', 'tp')
- attention_output_grad: bfloat16 [1536, 8192], P(None, 'seq')
- adapter_down_gradient: float32 [8192, 64], P('seq')
- adapter_up_gradient: float32 [64, 8192], P(None, 'tp')
- router_gate_gradient: float32 [1536], P('seq')
Inputs may be any that keep to these rules, and one draw needn't show every extreme that they name: `counts`: every shard has at least one live slot, all shards together have 768, and some shard has all 48 slots live. `selected`: within each shard's 48 slots the entries are distinct token positions of that shard; only the first counts entries of a shard are live.
All inputs are finite; a program needn't handle non-finite values.
Results may differ from a plain program's by a relative error of at most 0.0058.
Values may be sent and summed in bfloat16 or wider, within the bound.
A program may use at most 64 MiB of HBM per device.

v0:
```python
import jax
import jax.numpy as jnp
from jax import lax
from jax.sharding import PartitionSpec as P

LEVELS = (
    -1.0,
    -0.6961928009986877,
    -0.5250730514526367,
    -0.39491748809814453,
    -0.28444138169288635,
    -0.18477343022823334,
    -0.09105003625154495,
    0.0,
    0.07958029955625534,
    0.16093020141124725,
    0.24611230194568634,
    0.33791524171829224,
    0.44070982933044434,
    0.5626170039176941,
    0.7229568362236023,
    1.0,
)
adapter_scale = 0.25


def precise_matmul(left, right):
    return jnp.dot(left, right, precision=lax.Precision.HIGHEST, preferred_element_type=jnp.float32)


def dequantize(quantized_codes, absmax):
    quantile_levels = jnp.zeros(quantized_codes.shape, jnp.float32)
    for level_code in range(16):
        quantile_levels = quantile_levels + jnp.where(
            quantized_codes == level_code, LEVELS[level_code], 0.0
        )
    block_size = quantized_codes.shape[1] // absmax.shape[1]
    scales = jnp.repeat(absmax, block_size, axis=1)
    return (quantile_levels * scales).astype(jnp.bfloat16)


def body(
    residual,
    attention,
    quantized_codes,
    absmax,
    adapter_down,
    adapter_up,
    routed_slot_gate,
    selected,
    counts,
    cotangent,
):
    projection_weight = dequantize(quantized_codes, absmax)
    adapter_up_single32 = adapter_up.astype(jnp.float32)
    home_slots = attention.shape[0]
    live_slot = jnp.arange(home_slots, dtype=jnp.int32) < counts[0]
    target = jnp.where(live_slot, selected, residual.shape[0])
    full_w, full_a = (
        lax.all_gather(projection_weight, "seq", axis=0, tiled=True),
        lax.all_gather(adapter_down, "seq", axis=0, tiled=True),
    )
    adapter_product = jnp.dot(attention, full_a, preferred_element_type=jnp.float32)
    block_output = jnp.dot(
        attention, full_w, preferred_element_type=jnp.float32
    ) + adapter_scale * precise_matmul(adapter_product, adapter_up_single32)
    picked = residual[selected].astype(jnp.float32)
    updated = (picked + routed_slot_gate[:, None] * block_output).astype(jnp.bfloat16)
    outgoing_residual = residual.at[target].set(updated, mode="drop")
    upstream = jnp.where(live_slot[:, None], cotangent[selected].astype(jnp.float32), 0.0)
    gate_part = jnp.sum(upstream * block_output, axis=1)
    output_gradient = (routed_slot_gate[:, None] * upstream).astype(jnp.bfloat16)
    head_part = jnp.dot(output_gradient, full_w.T, preferred_element_type=jnp.float32)
    adapter_rank_piece = adapter_scale * jnp.dot(
        output_gradient, adapter_up.T, preferred_element_type=jnp.float32
    )
    head_full, rank_full, router_gate_gradient = lax.psum(
        (head_part, adapter_rank_piece, gate_part), "tp"
    )
    adapter_rank_gradient = rank_full.astype(jnp.bfloat16)
    home_grad = (
        head_full + jnp.dot(adapter_rank_gradient, full_a.T, preferred_element_type=jnp.float32)
    ).astype(jnp.bfloat16)
    attention_output_grad = lax.all_to_all(
        home_grad, "seq", split_axis=1, concat_axis=0, tiled=True
    )
    adapter_down_gradient = lax.psum_scatter(
        jnp.dot(attention.T, adapter_rank_gradient, preferred_element_type=jnp.float32),
        "seq",
        scatter_dimension=0,
        tiled=True,
    )
    up_factor_piece = adapter_scale * precise_matmul(
        adapter_product.T, output_gradient.astype(jnp.float32)
    )
    adapter_up_gradient = lax.psum(up_factor_piece, "seq")
    return (
        outgoing_residual,
        attention_output_grad,
        adapter_down_gradient,
        adapter_up_gradient,
        router_gate_gradient,
    )


def solution(mesh):
    return jax.shard_map(
        body,
        mesh=mesh,
        in_specs=(
            P("seq", "tp"),
            P("seq", None),
            P("seq", "tp"),
            P("seq", "tp"),
            P("seq", None),
            P(None, "tp"),
            P("seq"),
            P("seq"),
            P("seq"),
            P("seq", "tp"),
        ),
        out_specs=(P("seq", "tp"), P(None, "seq"), P("seq", None), P(None, "tp"), P("seq")),
        check_vma=False,
    )
```

profile of v0, /device:TPU:8, one launch (start us, length us, event | category | flops | bytes accessed | tf_op | source)
XLA Modules:
  0.0 714.8 jit_solution(8451295507987079360)
XLA Ops:
  7.2 0.0 copy-start
  7.2 0.0 copy-start.7
  7.2 0.0 copy-start.4
  7.2 0.0 copy-start.6
  7.2 0.0 all-gather.3.cloned.1.call-start
  7.3 1.3 copy.33
  8.6 2.2 fusion.2
  10.8 0.0 all-gather.3.cloned.1.call-update
  10.8 0.0 all-gather.5.cloned.1.call-start
  10.8 0.7 all-gather.5.cloned.1.call-update
  11.5 0.0 all-reduce.4.cloned.1.call-start
  12.2 0.0 copy-done.7
  12.3 0.0 copy-done.4
  12.3 0.7 gather_fusion
  13.0 0.0 copy-start.5
  13.0 113.0 %all-gather.3.cloned.1.call-done = bf16[8192,512]{0,1:T(8,128)(2,1)} async-done(((bf16[256,512]{0,1:T(8,128)(2,1)}), bf16[8192,512]{0,1:T(8,128)(2,1)}) %all-gather.3.cloned.1.call-update) | async-done | bytes 8388624 | tf_op jit(solution)/shard_map/all_gather | solution.py:60
  126.0 0.0 copy-done.6
  126.0 6.1 fusion.8
  132.1 0.0 all-reduce.4.cloned.1.call-update
  132.1 0.0 all-reduce.6.cloned.1.call-start
  132.2 0.0 copy-done.5
  132.2 0.2 convolution_multiply_fusion.2
  132.4 71.0 %all-gather.5.cloned.1.call-done = bf16[8192,64]{0,1:T(8,128)(2,1)} async-done(((bf16[256,64]{0,1:T(8,128)(2,1)}), bf16[8192,64]{0,1:T(8,128)(2,1)}) %all-gather.5.cloned.1.call-update) | async-done | bytes 1048592 | tf_op jit(solution)/shard_map/all_gather | solution.py:61
  203.4 0.0 copy-done
  203.4 1.6 fusion.9
  205.1 0.9 convolution_multiply_fusion
  206.0 0.0 all-reduce.6.cloned.1.call-update
  206.0 0.0 reduce-scatter.2.cloned.1.call-start
  206.1 6.0 convolution_bitcast_fusion.1
  212.1 0.3 multiply_reduce_fusion
  212.4 42.8 %all-reduce = (bf16[48,64]{1,0:T(8,128)(2,1)S(1)}, f32[48]{0:T(128)}) all-reduce(f32[48,64]{1,0:T(8,128)S(1)} %convolution_multiply_fusion.2, f32[48]{0:T(128)S(1)} %get-tuple-element.9), channel_id=1, replica_groups=mesh['seq'=32,'tp'=16] {'tp'}, use_global_device_ids=true, to_apply=%region_2.3 | all-reduce | flops 3120 | bytes 18816 | tf_op jit(solution)/shard_map/psum | solution.py:77
  255.2 1.8 convolution_bitcast_fusion
  257.0 0.0 reduce-scatter.2.cloned.1.call-update
  257.1 64.0 %all-reduce.4.cloned.1.call-done = f32[48,8192]{1,0:T(8,128)} async-done(((f32[48,8192]{1,0:T(8,128)}), f32[48,8192]{1,0:T(8,128)}) %all-reduce.4.cloned.1.call-update) | async-done | bytes 1572880 | tf_op jit(solution)/shard_map/psum | solution.py:77
  321.1 0.0 copy-done.1
  321.1 1.8 fusion
  322.8 0.0 copy-start.3
  322.9 0.9 copy.51
  323.8 9.3 %all-to-all-start = ((bf16[48,32,256]{2,0,1:T(8,128)(2,1)}), bf16[48,32,256]{2,0,1:T(8,128)(2,1)S(1)}, u32[]{:S(2)}, u32[]{:S(2)}) async-start(bf16[48,32,256]{2,0,1:T(8,128)(2,1)} %bitcast.28), calls=%async_computation | async-start | bytes 1572864 | tf_op jit(solution)/shard_map/all_to_all | solution.py:84
  333.1 0.0 copy-done.3
  333.1 1.2 scatter_custom_fusion
  334.3 0.0 copy-start.2
  334.3 23.0 %all-to-all-done = bf16[48,32,256]{2,0,1:T(8,128)(2,1)S(1)} async-done(((bf16[48,32,256]{2,0,1:T(8,128)(2,1)}), bf16[48,32,256]{2,0,1:T(8,128)(2,1)S(1)}, u32[]{:S(2)}, u32[]{:S(2)}) %all-to-all-start) | async-done | bytes 786464 | tf_op jit(solution)/shard_map/all_to_all | solution.py:84
  357.3 123.7 %all-reduce.6.cloned.1.call-done = f32[64,512]{1,0:T(8,128)} async-done(((f32[64,512]{1,0:T(8,128)}), f32[64,512]{1,0:T(8,128)}) %all-reduce.6.cloned.1.call-update) | async-done | bytes 131088 | tf_op jit(solution)/shard_map/psum | solution.py:96
  481.0 224.9 %reduce-scatter.2.cloned.1.call-done = f32[256,64]{0,1:T(8,128)} async-done(((f32[8192,64]{0,1:T(8,128)}), f32[256,64]{0,1:T(8,128)}) %reduce-scatter.2.cloned.1.call-update) | async-done | bytes 65552 | tf_op jit(solution)/shard_map/reduce_scatter | solution.py:87
  705.9 0.9 copy.59
  706.7 1.6 copy.60
  708.3 0.0 copy-done.2
  (4 shorter events, 0.0 us)
Async XLA Ops:
  7.2 196.3 %copy-start = (bf16[48,8192]{1,0:T(8,128)(2,1)S(1)}, bf16[48,8192]{1,0:T(8,128)(2,1)}, u32[]{:S(2)}) copy-start(bf16[48,8192]{1,0:T(8,128)(2,1)} %param.11) | copy-start | bytes 2359300
  7.2 5.1 copy-start.7
  7.2 5.1 copy-start.4
  7.2 118.8 %copy-start.6 = (f32[48]{0:T(128)S(1)}, f32[48]{0:T(128)}, u32[]{:S(2)}) copy-start(f32[48]{0:T(128)} %param.16) | copy-start | bytes 580
  7.2 118.8 %all-gather.3.cloned.1.call-start = ((), (), s32[]{:S(2)}) async-start(), calls=%async_computation.2 | async-start | bytes 8650752 | tf_op jit(solution)/shard_map/all_gather | solution.py:60
  10.8 192.6 %all-gather.5.cloned.1.call-start = ((), (), s32[]{:S(2)}) async-start(), calls=%async_computation.3 | async-start | bytes 1081344 | tf_op jit(solution)/shard_map/all_gather | solution.py:61
  11.5 309.5 %all-reduce.4.cloned.1.call-start = ((), (), s32[]{:S(2)}) async-start(), calls=%async_computation.4 | async-start | bytes 3145728 | tf_op jit(solution)/shard_map/psum | solution.py:77
  13.0 119.2 %copy-start.5 = (bf16[64,512]{1,0:T(8,128)(2,1)S(1)}, bf16[64,512]{1,0:T(8,128)(2,1)}, u32[]{:S(2)}) copy-start(bf16[64,512]{1,0:T(8,128)(2,1)} %param.15) | copy-start | bytes 196612
  132.1 348.8 %all-reduce.6.cloned.1.call-start = ((), (), s32[]{:S(2)}) async-start(), calls=%async_computation.6 | async-start | bytes 262144 | tf_op jit(solution)/shard_map/psum | solution.py:96
  206.0 499.8 %reduce-scatter.2.cloned.1.call-start = ((), (), s32[]{:S(2)}) async-start(), calls=%async_computation.5 | async-start | bytes 2162688 | tf_op jit(solution)/shard_map/reduce_scatter | solution.py:87
  255.2 65.8 %copy-start.1 = (bf16[8192,64]{0,1:T(8,128)(2,1)S(1)}, bf16[8192,64]{0,1:T(8,128)(2,1)}, u32[]{:S(2)}) copy-start(bf16[8192,64]{0,1:T(8,128)(2,1)} %all-gather.5.cloned.1.call-done) | copy-start | bytes 3145732
  322.8 10.2 %copy-start.3 = (bf16[192,512]{1,0:T(8,128)(2,1)S(1)}, bf16[192,512]{1,0:T(8,128)(2,1)}, u32[]{:S(2)}) copy-start(bf16[192,512]{1,0:T(8,128)(2,1)} %param.10) | copy-start | bytes 589828
  323.8 33.5 %all-to-all-start = ((bf16[48,32,256]{2,0,1:T(8,128)(2,1)}), bf16[48,32,256]{2,0,1:T(8,128)(2,1)S(1)}, u32[]{:S(2)}, u32[]{:S(2)}) async-start(bf16[48,32,256]{2,0,1:T(8,128)(2,1)} %bitcast.28), calls=%async_computation | async-start | bytes 1572864 | tf_op jit(solution)/shard_map/all_to_all | solution.py:84
  334.3 374.0 %copy-start.2 = (bf16[192,512]{1,0:T(8,128)(2,1)}, bf16[192,512]{1,0:T(8,128)(2,1)S(1)}, u32[]{:S(2)}) copy-start(bf16[192,512]{1,0:T(8,128)(2,1)S(1)} %scatter_custom_fusion) | copy-start | bytes 589828
Sparse Core Ops, SparseCore 0:
  11.7 114.2 all-gather.2
  129.0 74.3 all-gather.4
  205.8 115.2 all-reduce.3
  325.3 155.5 all-reduce.5
  485.8 220.0 reduce-scatter.1
where the time goes:
time: 715 us
  waiting for transfers between devices  620 us (87%)
  blocking collectives  42.8 us (6%)
  matrix products  18.8 us (3%)
  between operations  14.6 us (2%)
  starting transfers between devices  9.47 us (1%)
    reduce_scatter x1, waiting for transfers between devices, body(): lax.psum_scatter(jnp.dot(attention.T, adapter_rank_gradient, preferred_el...  225 us
    psum x1, waiting for transfers between devices, body(): adapter_up_gradient = lax.psum(up_factor_piece, 'seq')  124 us
    all_gather x1, waiting for transfers between devices, body(): lax.all_gather(projection_weight, 'seq', axis=0, tiled=True)  113 us
    all_gather x1, waiting for transfers between devices, body(): lax.all_gather(adapter_down, 'seq', axis=0, tiled=True)  71 us
    psum x1, waiting for transfers between devices, body(): lax.psum((head_part, adapter_rank_piece, gate_part), 'tp')  64 us
    psum x1, blocking collectives, body(): lax.psum((head_part, adapter_rank_piece, gate_part), 'tp')  42.8 us
    all_to_all x1, waiting for transfers between devices, body(): lax.all_to_all(home_grad, 'seq', split_axis=1, concat_axis=0, tiled=True)  23 us
  transfers between devices with their start and end apart: 6, of which 6 were waited for; matrix products, arithmetic and copies ran while one was open for 3% of the time, Pallas kernels for 0%

commit v1 on v0

--- a/solution.py
+++ b/solution.py
@@ -81,8 +81,9 @@
     home_grad = (
         head_full + jnp.dot(adapter_rank_gradient, full_a.T, preferred_element_type=jnp.float32)
     ).astype(jnp.bfloat16)
-    attention_output_grad = lax.all_to_all(
-        home_grad, "seq", split_axis=1, concat_axis=0, tiled=True
+    attention_output_grad = jnp.concatenate(
+        lax.all_to_all(jnp.stack(jnp.split(home_grad, lax.axis_size("seq"), axis=1)), "seq", 0, 0),
+        axis=0,
     )
     adapter_down_gradient = lax.psum_scatter(
         jnp.dot(attention.T, adapter_rank_gradient, preferred_element_type=jnp.float32),

time: 715 us -> 718 us (level)
  local copies, waits for them, and re-layouts: 5.41 us -> 24 us
  waiting for transfers between devices: 620 us -> 604 us
    unnamed x19 -> x50, local copies, waits for them, and re-layouts: 3.81 us -> 22.8 us
    psum x1, waiting for transfers between devices: 124 us -> 108 us  [body(): adapter_up_gradient = lax.psum(up_factor_piece, 'seq')]
  transfers between devices with their start and end apart: 6 -> 6, of which waited for: 6 -> 6; matrix products, arithmetic and copies ran while one was open for 3% -> 6% of each run, Pallas kernels for 0% -> 0%
where the time goes in v1:
time: 718 us; the launch traced here: 717 us
  waiting for transfers between devices  604 us (84%)
  blocking collectives  42.8 us (6%)
  local copies, waits for them, and re-layouts  24 us (3%)
  matrix products  18.8 us (3%)
  between operations  14.6 us (2%)
  starting transfers between devices  9.47 us (1%)
    reduce_scatter x1, waiting for transfers between devices, body(): lax.psum_scatter(jnp.dot(attention.T, adapter_rank_gradient, preferred_el...  225 us
    all_gather x1, waiting for transfers between devices, body(): lax.all_gather(projection_weight, 'seq', axis=0, tiled=True)  113 us
    psum x1, waiting for transfers between devices, body(): adapter_up_gradient = lax.psum(up_factor_piece, 'seq')  108 us
    all_gather x1, waiting for transfers between devices, body(): lax.all_gather(adapter_down, 'seq', axis=0, tiled=True)  71 us
    psum x1, waiting for transfers between devices, body(): lax.psum((head_part, adapter_rank_piece, gate_part), 'tp')  64 us
    psum x1, blocking collectives, body(): lax.psum((head_part, adapter_rank_piece, gate_part), 'tp')  42.8 us
    unnamed x50, local copies, waits for them, and re-layouts  22.8 us
    all_to_all x1, waiting for transfers between devices, body(): lax.all_to_all(jnp.stack(jnp.split(home_grad, lax.axis_size('seq'), axis=...  22.5 us
  transfers between devices with their start and end apart: 6, of which 6 were waited for; matrix products, arithmetic and copies ran while one was open for 6% of the time, Pallas kernels for 0%

profile of v1, /device:TPU:8, one launch (start us, length us, event | category | flops | bytes accessed | tf_op | source)
XLA Modules:
  0.0 717.3 jit_solution(18225648584615811446)
XLA Ops:
  7.3 1.3 copy.16
  8.6 2.2 fusion.2
  10.8 0.7 all-gather.5.cloned.1.call-update
  12.3 0.7 gather_fusion
  13.0 113.0 %all-gather.3.cloned.1.call-done = bf16[8192,512]{0,1:T(8,128)(2,1)} async-done(((bf16[256,512]{0,1:T(8,128)(2,1)}), bf16[8192,512]{0,1:T(8,128)(2,1)}) %all-gather.3.cloned.1.call-update) | async-done | bytes 8388624 | tf_op jit(solution)/shard_map/all_gather | solution.py:60
  126.0 6.1 fusion.8
  132.4 71.0 %all-gather.5.cloned.1.call-done = bf16[8192,64]{0,1:T(8,128)(2,1)} async-done(((bf16[256,64]{0,1:T(8,128)(2,1)}), bf16[8192,64]{0,1:T(8,128)(2,1)}) %all-gather.5.cloned.1.call-update) | async-done | bytes 1048592 | tf_op jit(solution)/shard_map/all_gather | solution.py:61
  203.4 1.6 fusion.9
  205.1 0.9 convolution_multiply_fusion
  206.1 6.0 convolution_bitcast_fusion.1
  212.4 42.8 %all-reduce = (bf16[48,64]{1,0:T(8,128)(2,1)S(1)}, f32[48]{0:T(128)}) all-reduce(f32[48,64]{1,0:T(8,128)S(1)} %convolution_multiply_fusion.2, f32[48]{0:T(128)S(1)} %get-tuple-element.9), channel_id=1, replica_groups=mesh['seq'=32,'tp'=16] {'tp'}, use_global_device_ids=true, to_apply=%region_2.3 | all-reduce | flops 3120 | bytes 18816 | tf_op jit(solution)/shard_map/psum | solution.py:77
  255.2 1.8 convolution_bitcast_fusion
  257.1 64.0 %all-reduce.4.cloned.1.call-done = f32[48,8192]{1,0:T(8,128)} async-done(((f32[48,8192]{1,0:T(8,128)}), f32[48,8192]{1,0:T(8,128)}) %all-reduce.4.cloned.1.call-update) | async-done | bytes 1572880 | tf_op jit(solution)/shard_map/psum | solution.py:77
  321.1 1.8 fusion
  322.9 0.6 constant_dynamic-update-slice_fusion.31
  323.5 0.6 constant_dynamic-update-slice_fusion.30
  324.1 0.6 constant_dynamic-update-slice_fusion.29
  324.7 0.6 constant_dynamic-update-slice_fusion.28
  325.3 0.6 constant_dynamic-update-slice_fusion.27
  325.9 0.6 constant_dynamic-update-slice_fusion.26
  326.5 0.6 constant_dynamic-update-slice_fusion.25
  327.1 0.6 constant_dynamic-update-slice_fusion.24
  327.7 0.6 constant_dynamic-update-slice_fusion.23
  328.4 0.6 constant_dynamic-update-slice_fusion.22
  329.0 0.6 constant_dynamic-update-slice_fusion.21
  329.6 0.6 constant_dynamic-update-slice_fusion.20
  330.2 0.6 constant_dynamic-update-slice_fusion.19
  330.8 0.6 constant_dynamic-update-slice_fusion.18
  331.4 0.6 constant_dynamic-update-slice_fusion.17
  335.1 0.6 constant_dynamic-update-slice_fusion.11
  335.7 0.6 constant_dynamic-update-slice_fusion.10
  336.3 0.6 constant_dynamic-update-slice_fusion.9
  336.9 0.6 constant_dynamic-update-slice_fusion.8
  337.5 0.6 constant_dynamic-update-slice_fusion.7
  338.1 0.6 constant_dynamic-update-slice_fusion.6
  338.8 0.6 constant_dynamic-update-slice_fusion.5
  339.4 0.6 constant_dynamic-update-slice_fusion.4
  340.0 0.6 constant_dynamic-update-slice_fusion.3
  340.6 0.6 constant_dynamic-update-slice_fusion.2
  341.2 0.6 constant_dynamic-update-slice_fusion.1
  341.8 0.6 constant_dynamic-update-slice_fusion
  342.4 9.3 %all-to-all-start = ((bf16[32,48,256]{2,1,0:T(8,128)(2,1)}), bf16[32,48,256]{2,1,0:T(8,128)(2,1)S(1)}, u32[]{:S(2)}, u32[]{:S(2)}) async-start(bf16[32,48,256]{2,1,0:T(8,128)(2,1)} %constant_dynamic-update-slice_fusion), calls=%async_computation | async-start | bytes 1572864 | tf_op jit(solution)/shard_map/all_to_all | solution.py:85
  351.7 1.2 scatter_custom_fusion
  352.9 22.5 %all-to-all-done = bf16[32,48,256]{2,1,0:T(8,128)(2,1)S(1)} async-done(((bf16[32,48,256]{2,1,0:T(8,128)(2,1)}), bf16[32,48,256]{2,1,0:T(8,128)(2,1)S(1)}, u32[]{:S(2)}, u32[]{:S(2)}) %all-to-all-start) | async-done | bytes 786464 | tf_op jit(solution)/shard_map/all_to_all | solution.py:85
  375.5 108.0 %all-reduce.6.cloned.1.call-done = f32[64,512]{1,0:T(8,128)} async-done(((f32[64,512]{1,0:T(8,128)}), f32[64,512]{1,0:T(8,128)}) %all-reduce.6.cloned.1.call-update) | async-done | bytes 131088 | tf_op jit(solution)/shard_map/psum | solution.py:97
  483.5 224.9 %reduce-scatter.2.cloned.1.call-done = f32[256,64]{0,1:T(8,128)} async-done(((f32[8192,64]{0,1:T(8,128)}), f32[256,64]{0,1:T(8,128)}) %reduce-scatter.2.cloned.1.call-update) | async-done | bytes 65552 | tf_op jit(solution)/shard_map/reduce_scatter | solution.py:88
  708.4 0.9 copy.69
  709.2 1.6 copy.70
  (35 shorter events, 3.9 us)
Async XLA Ops:
  7.2 196.3 %copy-start = (bf16[48,8192]{1,0:T(8,128)(2,1)S(1)}, bf16[48,8192]{1,0:T(8,128)(2,1)}, u32[]{:S(2)}) copy-start(bf16[48,8192]{1,0:T(8,128)(2,1)} %param.11) | copy-start | bytes 2359300
  7.2 5.1 copy-start.7
  7.2 5.1 copy-start.4
  7.2 118.8 %copy-start.6 = (f32[48]{0:T(128)S(1)}, f32[48]{0:T(128)}, u32[]{:S(2)}) copy-start(f32[48]{0:T(128)} %param.16) | copy-start | bytes 580
  7.2 118.8 %all-gather.3.cloned.1.call-start = ((), (), s32[]{:S(2)}) async-start(), calls=%async_computation.2 | async-start | bytes 8650752 | tf_op jit(solution)/shard_map/all_gather | solution.py:60
  10.8 192.6 %all-gather.5.cloned.1.call-start = ((), (), s32[]{:S(2)}) async-start(), calls=%async_computation.3 | async-start | bytes 1081344 | tf_op jit(solution)/shard_map/all_gather | solution.py:61
  11.5 309.5 %all-reduce.4.cloned.1.call-start = ((), (), s32[]{:S(2)}) async-start(), calls=%async_computation.4 | async-start | bytes 3145728 | tf_op jit(solution)/shard_map/psum | solution.py:77
  13.0 119.2 %copy-start.5 = (bf16[64,512]{1,0:T(8,128)(2,1)S(1)}, bf16[64,512]{1,0:T(8,128)(2,1)}, u32[]{:S(2)}) copy-start(bf16[64,512]{1,0:T(8,128)(2,1)} %param.15) | copy-start | bytes 196612
  132.1 351.3 %all-reduce.6.cloned.1.call-start = ((), (), s32[]{:S(2)}) async-start(), calls=%async_computation.6 | async-start | bytes 262144 | tf_op jit(solution)/shard_map/psum | solution.py:97
  206.0 502.3 %reduce-scatter.2.cloned.1.call-start = ((), (), s32[]{:S(2)}) async-start(), calls=%async_computation.5 | async-start | bytes 2162688 | tf_op jit(solution)/shard_map/reduce_scatter | solution.py:88
  255.2 65.8 %copy-start.1 = (bf16[8192,64]{0,1:T(8,128)(2,1)S(1)}, bf16[8192,64]{0,1:T(8,128)(2,1)}, u32[]{:S(2)}) copy-start(bf16[8192,64]{0,1:T(8,128)(2,1)} %all-gather.5.cloned.1.call-done) | copy-start | bytes 3145732
  322.8 28.9 %copy-start.3 = (bf16[192,512]{1,0:T(8,128)(2,1)S(1)}, bf16[192,512]{1,0:T(8,128)(2,1)}, u32[]{:S(2)}) copy-start(bf16[192,512]{1,0:T(8,128)(2,1)} %param.10) | copy-start | bytes 589828
  342.4 33.0 %all-to-all-start = ((bf16[32,48,256]{2,1,0:T(8,128)(2,1)}), bf16[32,48,256]{2,1,0:T(8,128)(2,1)S(1)}, u32[]{:S(2)}, u32[]{:S(2)}) async-start(bf16[32,48,256]{2,1,0:T(8,128)(2,1)} %constant_dynamic-update-slice_fusion), calls=%async_computation | async-start | bytes 1572864 | tf_op jit(solution)/shard_map/all_to_all | solution.py:85
  352.9 357.9 %copy-start.2 = (bf16[192,512]{1,0:T(8,128)(2,1)}, bf16[192,512]{1,0:T(8,128)(2,1)S(1)}, u32[]{:S(2)}) copy-start(bf16[192,512]{1,0:T(8,128)(2,1)S(1)} %scatter_custom_fusion) | copy-start | bytes 589828
Sparse Core Ops, SparseCore 0:
  11.7 114.2 all-gather.2
  129.0 74.3 all-gather.4
  205.8 115.2 all-reduce.3
  325.3 158.0 all-reduce.5
  488.3 220.0 reduce-scatter.1
